TPU v7x, 32 devices: a whole 2x2x4 slice. The times are simulated.
32 devices in a mesh: row: 8 (over y, x, core), col: 4 (over z).
Axes of the slice: x: 2, y: 2, z: 4, core: 2. Of those that a mesh axis runs over, the one named last changes fastest.
Arguments:
- matrix: float32 [16384, 16384], P('row', 'col'), may hold values from -8 to 8, as said below
- vectors: float32 [16384, 8192], P('row', 'col'), may hold values from -6 to 6
Outputs:
- updated: float32 [16384, 16384], P('row', 'col')
- rotated: float32 [16384, 8192], P('row', 'col')
Inputs may be any that keep to these rules, and one draw needn't show every extreme that they name: matrix is symmetric up to rounding.
All inputs are finite; a program needn't handle non-finite values.
Results may differ from a plain program's by a relative error of at most 0.00011.
Values sent between devices are 32-bit elements; how exact they have to be, the bound alone decides.
A program may use at most 192 MiB of HBM per device.

v0:
```python
import jax
import jax.numpy as jnp
from jax import lax
from jax.sharding import PartitionSpec as P

B = 256


def broadcast(array, axis, root):
    mine = lax.axis_index(axis) == root
    return lax.psum(jnp.where(mine, array, jnp.zeros_like(array)), axis)


def matmul(left, right):
    return jnp.dot(left, right, preferred_element_type=jnp.float32, precision=lax.Precision.HIGHEST)


def inner_product(left, right):
    return lax.dot_general(
        left,
        right,
        (((0,), (0,)), ((), ())),
        preferred_element_type=jnp.float32,
        precision=lax.Precision.HIGHEST,
    )


def outer_product(left, right):
    return lax.dot_general(
        left,
        right,
        (((1,), (1,)), ((), ())),
        preferred_element_type=jnp.float32,
        precision=lax.Precision.HIGHEST,
    )


def body(matrix, vectors):
    rows_here = matrix.shape[0]
    columns_here = matrix.shape[1]
    row_index = lax.axis_index("row")
    column_index = lax.axis_index("col")
    row_panel = broadcast(matrix[:, :B], "col", 0)
    column_panel = broadcast(matrix[:B, :], "row", 0)
    global_rows = row_index * rows_here + jnp.arange(rows_here, dtype=jnp.int32)
    global_columns = column_index * columns_here + jnp.arange(columns_here, dtype=jnp.int32)
    row_panel = jnp.where(global_rows[:, None] >= B, row_panel, jnp.float32(0.0))
    column_panel = jnp.where(global_columns[None, :] >= B, column_panel, jnp.float32(0.0))
    gram = lax.psum(inner_product(row_panel, row_panel), "row")
    factor = jnp.linalg.cholesky(gram)
    basis_rows = lax.linalg.triangular_solve(
        factor, row_panel, left_side=False, lower=True, transpose_a=True
    )
    basis_columns = lax.linalg.triangular_solve(
        factor, column_panel.T, left_side=False, lower=True, transpose_a=True
    )
    product_rows = lax.psum(matmul(matrix, basis_columns), "col")
    product_columns = lax.psum(inner_product(matrix, basis_rows), "row")
    coupling = lax.psum(inner_product(basis_rows, product_rows), "row")
    wide_rows = 2.0 * product_rows - 2.0 * matmul(basis_rows, coupling)
    wide_columns = 2.0 * product_columns - 2.0 * matmul(basis_columns, coupling)
    updated = (
        matrix - outer_product(basis_rows, wide_columns) - outer_product(wide_rows, basis_columns)
    )
    mixing = lax.psum(inner_product(basis_rows, vectors), "row")
    rotated = vectors - 2.0 * matmul(basis_rows, mixing)
    return (updated, rotated)


def solution(mesh):
    placed = (P("row", "col"), P("row", "col"))
    return jax.shard_map(
        body,
        mesh=mesh,
        in_specs=placed,
        out_specs=(P("row", "col"), P("row", "col")),
        check_vma=False,
    )
```

profile of v0, /device:TPU:0, one launch (start us, length us, event | category | flops | bytes accessed | tf_op | source)
XLA Modules:
  0.0 605.2 jit_solution(10097662528827411280)
XLA Ops:
  7.2 3.0 slice_select_fusion.1
  10.4 4.6 slice_select_fusion
  15.0 84.8 %all-reduce.8.cloned.1.call-done = f32[2048,256]{1,0:T(8,128)} async-done(((f32[2048,256]{1,0:T(8,128)}), f32[2048,256]{1,0:T(8,128)}) %all-reduce.8.cloned.1.call-update) | async-done | bytes 2097168 | tf_op jit(solution)/shard_map/psum | solution.py:11
  99.8 1.9 broadcast_select_fusion
  101.7 4.2 fusion.27
  106.5 82.4 %all-reduce.14.cloned.1.call-done = (f32[256,4096]{1,0:T(8,128)}, f32[256,256]{0,1:T(8,128)}) async-done(((f32[256,4096]{1,0:T(8,128)}, f32[256,256]{0,1:T(8,128)}), (f32[256,4096]{1,0:T(8,128)}, f32[256,256]{0,1:T(8,128)})) %all-reduce.14.cloned.1.call-update) | async-done | bytes 4456464 | tf_op jit(solution)/shard_map/psum | solution.py:11
  188.8 1.1 copy.5
  190.9 11.7 %cholesky.50 = f32[128,128]{1,0:T(8,128)S(1)} custom-call(f32[128,128]{1,0:T(8,128)S(1)} %cholesky.118), custom_call_target="Cholesky" | custom-call | tf_op jit(solution)/shard_map/jit(cholesky)/cholesky | solution.py:50
  202.7 9.8 %custom-call.16 = f32[1,128,128]{1,2,0:T(8,128)S(1)} custom-call(f32[1,128,128]{2,1,0:T(8,128)S(1)} %get-tuple-element.28), custom_call_target="InvertDiagBlocksLowerTriangular" | custom-call | tf_op jit(solution)/shard_map/jit(cholesky)/cholesky | solution.py:50
  213.0 11.7 %cholesky.105 = f32[128,128]{1,0:T(8,128)S(1)} custom-call(f32[128,128]{1,0:T(8,128)S(1)} %convolution_subtract_fusion.2), custom_call_target="Cholesky" | custom-call | tf_op jit(solution)/shard_map/jit(cholesky)/cholesky | solution.py:50
  226.8 4.0 while.1
  227.4 1.4 bitcast_dynamic-update-slice_fusion.2
  229.4 1.4 bitcast_dynamic-update-slice_fusion.2
  230.8 19.8 %custom-call.17 = f32[2,128,128]{1,2,0:T(8,128)S(1)} custom-call(f32[2,128,128]{2,1,0:T(8,128)S(1)} %get-tuple-element.9), custom_call_target="InvertDiagBlocksLowerTriangular" | custom-call | tf_op jit(solution)/shard_map/triangular_solve | solution.py:51
  250.6 1.1 fusion.4
  251.7 1.8 convolution_subtract_fusion.1
  253.6 2.1 fusion.14
  256.1 2.0 fusion.2
  258.1 2.1 convolution_subtract_fusion
  260.2 2.0 fusion.13
  262.2 1.3 copy-done.2
  263.5 34.5 %convolution_bitcast_fusion.1 = f32[2048,256]{0,1:T(8,128)} fusion(f32[2048,4096]{1,0:T(8,128)} %param.2, f32[4096,128]{0,1:T(8,128)S(1)} %fusion.13, f32[4096,128]{0,1:T(8,128)S(1)} %fusion.2), kind=kOutput, calls=%fused_computation.13 | convolution fusion | flops 25770852352 | bytes 39845888 | tf_op jit(solution)/shard_map/dot_general | solution.py:15
  298.1 18.2 %fusion.7 = f32[256,2048]{1,0:T(8,128)} fusion(f32[2048,2048]{1,0:T(8,128)} %param.3, f32[2048,128]{0,1:T(8,128)} %fusion.14, f32[2048,128]{0,1:T(8,128)S(1)} %fusion.4), kind=kOutput, calls=%fused_computation.27 | convolution fusion | flops 12885426176 | bytes 20971520 | tf_op jit(solution)/shard_map/dot_general | solution.py:19
  316.4 33.8 %convolution_bitcast_fusion = f32[4096,256]{0,1:T(8,128)} fusion(f32[2048,4096]{1,0:T(8,128)} %param.2, f32[2048,128]{0,1:T(8,128)S(1)} %copy-done, f32[2048,128]{0,1:T(8,128)S(1)} %fusion.4), kind=kOutput, calls=%fused_computation.6 | convolution fusion | flops 25770328064 | bytes 39845888 | tf_op jit(solution)/shard_map/dot_general | solution.py:19
  350.2 34.2 %all-reduce.10.cloned.1.call-done = f32[2048,256]{0,1:T(8,128)} async-done(((f32[2048,256]{0,1:T(8,128)}), f32[2048,256]{0,1:T(8,128)}) %all-reduce.10.cloned.1.call-update) | async-done | bytes 2097168 | tf_op jit(solution)/shard_map/psum | solution.py:57
  384.4 4.5 fusion.9
  388.9 106.1 %all-reduce.12.cloned.1.call-done = (f32[256,256]{1,0:T(8,128)}, f32[4096,256]{0,1:T(8,128)}, f32[256,2048]{1,0:T(8,128)}) async-done(((f32[256,256]{1,0:T(8,128)}, f32[4096,256]{0,1:T(8,128)}, f32[256,2048]{1,0:T(8,128)}), (f32[256,256]{1,0:T(8,128)}, f32[4096,256]{0,1:T(8,128)}, f32[256,2048]{1,0:T(8,128)})) %all-reduce.12.cloned.1.call-update) | async-done | bytes 6553616 | tf_op jit(solution)/shard_map/psum | solution.py:59
  495.0 7.3 %fusion = f32[4096,256]{0,1:T(8,128)S(1)} fusion(f32[256,256]{1,0:T(8,128)} %get-tuple-element.18, f32[4096,256]{0,1:T(8,128)} %get-tuple-element.19, f32[4096,128]{0,1:T(8,128)} %copy-done.2, f32[4096,128]{0,1:T(8,128)S(1)} %fusion.2), kind=kOutput, calls=%fused_computation.5 | convolution fusion | flops 3225419776 | bytes 12845056 | tf_op jit(solution)/shard_map/dot_general | solution.py:15
  502.3 30.7 %fusion.8 = f32[2048,4096]{1,0:T(8,128)} fusion(f32[4096,256]{0,1:T(8,128)S(1)} %fusion, f32[2048,128]{0,1:T(8,128)S(1)} %copy-done.1, f32[2048,128]{0,1:T(8,128)S(1)} %fusion.4), kind=kOutput, calls=%fused_computation.28 | convolution fusion | flops 25770328064 | bytes 39845888 | tf_op jit(solution)/shard_map/dot_general | solution.py:29
  533.0 19.2 %multiply_subtract_fusion = f32[2048,2048]{1,0:T(8,128)} fusion(f32[2048,2048]{1,0:T(8,128)} %param.3, f32[256,2048]{1,0:T(8,128)S(1)} %copy-done.5, f32[2048,128]{0,1:T(8,128)S(1)} %copy-done.1, f32[2048,128]{0,1:T(8,128)S(1)} %fusion.4), kind=kOutput, calls=%fused_computation.3 | convolution fusion | flops 12893814784 | bytes 37748736 | tf_op jit(solution)/shard_map/dot_general | solution.py:15
  552.3 3.5 fusion.1
  555.8 42.6 %subtract_subtract_fusion = f32[2048,4096]{1,0:T(8,128)} fusion(f32[2048,4096]{1,0:T(8,128)} %param.2, f32[2048,4096]{1,0:T(8,128)} %fusion.8, f32[2048,256]{0,1:T(8,128)} %fusion.1, f32[4096,128]{0,1:T(8,128)} %copy-done.2, f32[4096,128]{0,1:T(8,128)S(1)} %fusion.2), kind=kOutput, calls=%fused_computation.2 | convolution fusion | flops 25787629568 | bytes 106954752 | tf_op jit(solution)/shard_map/dot_general | solution.py:29
  (40 shorter events, 4.7 us)
Async XLA Ops:
  7.2 92.6 %all-reduce.8.cloned.1.call-start = ((), (), s32[]{:S(2)}) async-start(), calls=%async_computation | async-start | bytes 4194304 | tf_op jit(solution)/shard_map/psum | solution.py:11
  10.3 178.5 %all-reduce.14.cloned.1.call-start = ((), (), s32[]{:S(2)}) async-start(), calls=%async_computation.3 | async-start | bytes 8912896 | tf_op jit(solution)/shard_map/psum | solution.py:11
  105.9 278.5 %all-reduce.10.cloned.1.call-start = ((), (), s32[]{:S(2)}) async-start(), calls=%async_computation.1 | async-start | bytes 4194304 | tf_op jit(solution)/shard_map/psum | solution.py:57
  251.7 3.9 copy-start.4
  262.2 1.3 copy-start.2
  298.1 196.9 %all-reduce.12.cloned.1.call-start = ((), (), s32[]{:S(2)}) async-start(), calls=%async_computation.2 | async-start | bytes 13107200 | tf_op jit(solution)/shard_map/psum | solution.py:59
  298.1 18.3 %copy-start = (f32[2048,128]{0,1:T(8,128)S(1)}, f32[2048,128]{0,1:T(8,128)}, u32[]{:S(2)}) copy-start(f32[2048,128]{0,1:T(8,128)} %fusion.14) | copy-start | bytes 3145732
  495.0 7.3 %copy-start.1 = (f32[2048,128]{0,1:T(8,128)S(1)}, f32[2048,128]{0,1:T(8,128)}, u32[]{:S(2)}) copy-start(f32[2048,128]{0,1:T(8,128)} %fusion.14) | copy-start | bytes 3145732
  502.3 30.7 %copy-start.5 = (f32[256,2048]{1,0:T(8,128)S(1)}, f32[256,2048]{1,0:T(8,128)}, u32[]{:S(2)}) copy-start(f32[256,2048]{1,0:T(8,128)} %get-tuple-element.20) | copy-start | bytes 6291460
  533.0 19.3 %copy-start.3 = (f32[2048,256]{0,1:T(8,128)S(1)}, f32[2048,256]{0,1:T(8,128)}, u32[]{:S(2)}) copy-start(f32[2048,256]{0,1:T(8,128)} %all-reduce.10.cloned.1.call-done) | copy-start | bytes 6291460
  533.0 19.3 %copy-start.6 = (f32[256,256]{1,0:T(8,128)S(1)}, f32[256,256]{1,0:T(8,128)}, u32[]{:S(2)}) copy-start(f32[256,256]{1,0:T(8,128)} %get-tuple-element.18) | copy-start | bytes 786436
Sparse Core Ops, SparseCore 0:
  10.9 88.8 all-reduce.7
  106.0 82.7 all-reduce.13
  298.2 86.1 all-reduce.9
  389.0 105.9 all-reduce.11
where the time goes:
time: 609 us; the launch traced here: 605 us
  waiting for transfers between devices  308 us (51%)
  matrix products  210 us (34%)
  other arithmetic  64.9 us (11%)
  between operations  15.5 us (3%)
  local copies, waits for them, and re-layouts  6.46 us (1%)
    psum x2, waiting for transfers between devices, broadcast(): return lax.psum(jnp.where(mine, array, jnp.zeros_like(array)), axis)  167 us
    psum x1, waiting for transfers between devices, body(): coupling = lax.psum(inner_product(basis_rows, product_rows), 'row')  106 us
    dot_general x2, matrix products, outer_product(): lax.dot_general(left, right, (((1,), (1,)), ((), ())), preferred_element_...  73.4 us
    dot_general x4, matrix products, matmul(): jnp.dot(left, right, preferred_element_type=jnp.float32, precision=lax.Pr...  64.5 us
    dot_general x4, matrix products, inner_product(): lax.dot_general(left, right, (((0,), (0,)), ((), ())), preferred_element_...  60.7 us
    psum x1, waiting for transfers between devices, body(): product_rows = lax.psum(matmul(matrix, basis_columns), 'col')  34.2 us
    another operation x6, other arithmetic, body(): factor = jnp.linalg.cholesky(gram)  34 us
    another operation x3, other arithmetic, body(): lax.linalg.triangular_solve(factor, row_panel, left_side=False, lower=Tru...  19.9 us
  transfers between devices with their start and end apart: 4, of which 4 were waited for; matrix products, arithmetic and copies ran while one was open for 9% of the time, Pallas kernels for 0%

commit v1 on v0

--- a/solution.py
+++ b/solution.py
@@ -8,7 +8,11 @@
 
 def broadcast(array, axis, root):
     mine = lax.axis_index(axis) == root
-    return lax.psum(jnp.where(mine, array, jnp.zeros_like(array)), axis)
+
+    def units_state(block_here, group_axis):
+        return jnp.sum(lax.all_gather(block_here, axis_name=group_axis), axis=0)
+
+    return units_state(jnp.where(mine, array, jnp.zeros_like(array)), axis)
 
 
 def matmul(left, right):

time: 609 us -> 760 us (1.25)
  waiting for transfers between devices: 308 us -> 434 us
  other arithmetic: 64.9 us -> 86.5 us
    all_gather x0 -> x2, waiting for transfers between devices: none -> 248 us  [units_state(): return jnp.sum(lax.all_gather(block_here, axis_name=group_axis), axis=0)]
    psum x2 -> x1, waiting for transfers between devices: 167 us -> 47.1 us  [body(): gram = lax.psum(inner_product(row_panel, row_panel), 'row')]
    reduce_sum x0 -> x2, other arithmetic: none -> 19.7 us  [units_state(): return jnp.sum(lax.all_gather(block_here, axis_name=group_axis), axis=0)]
  transfers between devices with their start and end apart: 4 -> 5, of which waited for: 4 -> 5; matrix products, arithmetic and copies ran while one was open for 9% -> 16% of each run, Pallas kernels for 0% -> 0%
where the time goes in v1:
time: 760 us; the launch traced here: 755 us
  waiting for transfers between devices  434 us (57%)
  matrix products  211 us (28%)
  other arithmetic  86.5 us (11%)
  between operations  15.5 us (2%)
    all_gather x2, waiting for transfers between devices, units_state(): return jnp.sum(lax.all_gather(block_here, axis_name=group_axis), axis=0)  248 us
    psum x1, waiting for transfers between devices, body(): coupling = lax.psum(inner_product(basis_rows, product_rows), 'row')  106 us
    dot_general x2, matrix products, outer_product(): lax.dot_general(left, right, (((1,), (1,)), ((), ())), preferred_element_...  73.6 us
    dot_general x4, matrix products, matmul(): jnp.dot(left, right, preferred_element_type=jnp.float32, precision=lax.Pr...  64.3 us
    dot_general x4, matrix products, inner_product(): lax.dot_general(left, right, (((0,), (0,)), ((), ())), preferred_element_...  61.6 us
    psum x1, waiting for transfers between devices, body(): gram = lax.psum(inner_product(row_panel, row_panel), 'row')  47.1 us
    another operation x6, other arithmetic, body(): factor = jnp.linalg.cholesky(gram)  34 us
    psum x1, waiting for transfers between devices, body(): product_rows = lax.psum(matmul(matrix, basis_columns), 'col')  33.3 us
  transfers between devices with their start and end apart: 5, of which 5 were waited for; matrix products, arithmetic and copies ran while one was open for 16% of the time, Pallas kernels for 0%

profile of v1, /device:TPU:0, one launch (start us, length us, event | category | flops | bytes accessed | tf_op | source)
XLA Modules:
  0.0 754.9 jit_solution(15186846126392545861)
XLA Ops:
  7.2 3.0 slice_select_fusion.1
  10.4 152.4 %all-gather.5.cloned.1.call-done = f32[8192,256]{1,0:T(8,128)} async-done(((f32[2048,256]{1,0:T(8,128)}), f32[8192,256]{1,0:T(8,128)}) %all-gather.5.cloned.1.call-update) | async-done | bytes 8388624 | tf_op jit(solution)/shard_map/all_gather | solution.py:13
  162.8 5.5 reduce_sum.18
  168.3 1.9 broadcast_select_fusion
  170.2 4.2 fusion.27
  174.5 4.6 slice_select_fusion
  179.5 47.1 %all-reduce.6.cloned.1.call-done = f32[256,256]{0,1:T(8,128)} async-done(((f32[256,256]{0,1:T(8,128)}), f32[256,256]{0,1:T(8,128)}) %all-reduce.6.cloned.1.call-update) | async-done | bytes 262160 | tf_op jit(solution)/shard_map/psum | solution.py:53
  228.7 11.7 %cholesky.50 = f32[128,128]{1,0:T(8,128)S(1)} custom-call(f32[128,128]{1,0:T(8,128)S(1)} %cholesky.118), custom_call_target="Cholesky" | custom-call | tf_op jit(solution)/shard_map/jit(cholesky)/cholesky | solution.py:54
  240.5 9.8 %custom-call.16 = f32[1,128,128]{1,2,0:T(8,128)S(1)} custom-call(f32[1,128,128]{2,1,0:T(8,128)S(1)} %get-tuple-element.26), custom_call_target="InvertDiagBlocksLowerTriangular" | custom-call | tf_op jit(solution)/shard_map/jit(cholesky)/cholesky | solution.py:54
  250.8 11.7 %cholesky.105 = f32[128,128]{1,0:T(8,128)S(1)} custom-call(f32[128,128]{1,0:T(8,128)S(1)} %convolution_subtract_fusion.2), custom_call_target="Cholesky" | custom-call | tf_op jit(solution)/shard_map/jit(cholesky)/cholesky | solution.py:54
  264.7 4.4 while.1
  265.8 1.4 bitcast_dynamic-update-slice_fusion.2
  269.1 19.7 %custom-call.17 = f32[2,128,128]{1,2,0:T(8,128)S(1)} custom-call(f32[2,128,128]{2,1,0:T(8,128)S(1)} %get-tuple-element.9), custom_call_target="InvertDiagBlocksLowerTriangular" | custom-call | tf_op jit(solution)/shard_map/triangular_solve | solution.py:55
  289.9 1.8 convolution_subtract_fusion.1
  291.7 2.1 fusion.14
  293.8 95.5 %all-gather.7.cloned.1.call-done = f32[2048,4096]{1,0:T(8,128)} async-done(((f32[256,4096]{1,0:T(8,128)}), f32[2048,4096]{1,0:T(8,128)}) %all-gather.7.cloned.1.call-update) | async-done | bytes 33554448 | tf_op jit(solution)/shard_map/all_gather | solution.py:13
  389.2 14.2 %reduce_sum.19 = f32[256,4096]{1,0:T(8,128)} reduce(f32[8,256,4096]{2,1,0:T(8,128)} %bitcast.54, f32[]{:T(128)} %constant.100.clone.1), dimensions={0}, to_apply=%region_7.8 | reduce | flops 7340032 | bytes 37748740 | tf_op jit(solution)/shard_map/reduce_sum | solution.py:13
  403.4 2.5 select_bitcast_fusion
  405.9 2.0 fusion.2
  407.9 2.1 convolution_subtract_fusion
  410.0 2.0 fusion.13
  413.3 34.3 %convolution_bitcast_fusion.1 = f32[2048,256]{0,1:T(8,128)} fusion(f32[2048,4096]{1,0:T(8,128)} %param.2, f32[4096,128]{0,1:T(8,128)S(1)} %fusion.13, f32[4096,128]{0,1:T(8,128)S(1)} %fusion.2), kind=kOutput, calls=%fused_computation.13 | convolution fusion | flops 25770852352 | bytes 39845888 | tf_op jit(solution)/shard_map/dot_general | solution.py:19
  447.7 19.2 %fusion.7 = f32[256,2048]{1,0:T(8,128)} fusion(f32[2048,2048]{1,0:T(8,128)} %param.3, f32[2048,128]{0,1:T(8,128)} %fusion.14, f32[2048,128]{0,1:T(8,128)S(1)} %fusion.4), kind=kOutput, calls=%fused_computation.27 | convolution fusion | flops 12885426176 | bytes 20971520 | tf_op jit(solution)/shard_map/dot_general | solution.py:23
  466.9 33.7 %convolution_bitcast_fusion = f32[4096,256]{0,1:T(8,128)} fusion(f32[2048,4096]{1,0:T(8,128)} %param.2, f32[2048,128]{0,1:T(8,128)S(1)} %copy-done, f32[2048,128]{0,1:T(8,128)S(1)} %fusion.4), kind=kOutput, calls=%fused_computation.6 | convolution fusion | flops 25770328064 | bytes 39845888 | tf_op jit(solution)/shard_map/dot_general | solution.py:23
  500.7 33.3 %all-reduce.8.cloned.1.call-done = f32[2048,256]{0,1:T(8,128)} async-done(((f32[2048,256]{0,1:T(8,128)}), f32[2048,256]{0,1:T(8,128)}) %all-reduce.8.cloned.1.call-update) | async-done | bytes 2097168 | tf_op jit(solution)/shard_map/psum | solution.py:61
  533.9 4.5 fusion.9
  538.4 106.1 %all-reduce.10.cloned.1.call-done = (f32[256,256]{1,0:T(8,128)}, f32[4096,256]{0,1:T(8,128)}, f32[256,2048]{1,0:T(8,128)}) async-done(((f32[256,256]{1,0:T(8,128)}, f32[4096,256]{0,1:T(8,128)}, f32[256,2048]{1,0:T(8,128)}), (f32[256,256]{1,0:T(8,128)}, f32[4096,256]{0,1:T(8,128)}, f32[256,2048]{1,0:T(8,128)})) %all-reduce.10.cloned.1.call-update) | async-done | bytes 6553616 | tf_op jit(solution)/shard_map/psum | solution.py:63
  644.5 7.3 fusion
  651.8 31.0 %fusion.8 = f32[2048,4096]{1,0:T(8,128)} fusion(f32[4096,256]{0,1:T(8,128)S(1)} %fusion, f32[2048,128]{0,1:T(8,128)S(1)} %copy-done.1, f32[2048,128]{0,1:T(8,128)S(1)} %fusion.4), kind=kOutput, calls=%fused_computation.28 | convolution fusion | flops 25770328064 | bytes 39845888 | tf_op jit(solution)/shard_map/dot_general | solution.py:33
  682.8 19.2 %multiply_subtract_fusion = f32[2048,2048]{1,0:T(8,128)} fusion(f32[2048,2048]{1,0:T(8,128)} %param.3, f32[256,2048]{1,0:T(8,128)S(1)} %copy-done.4, f32[2048,128]{0,1:T(8,128)S(1)} %copy-done.1, f32[2048,128]{0,1:T(8,128)S(1)} %fusion.4), kind=kOutput, calls=%fused_computation.3 | convolution fusion | flops 12893814784 | bytes 37748736 | tf_op jit(solution)/shard_map/dot_general | solution.py:19
  702.1 3.5 fusion.1
  705.6 42.6 %subtract_subtract_fusion = f32[2048,4096]{1,0:T(8,128)} fusion(f32[2048,4096]{1,0:T(8,128)} %param.2, f32[2048,4096]{1,0:T(8,128)} %fusion.8, f32[2048,256]{0,1:T(8,128)} %fusion.1, f32[4096,128]{0,1:T(8,128)} %copy-done.2, f32[4096,128]{0,1:T(8,128)S(1)} %fusion.2), kind=kOutput, calls=%fused_computation.2 | convolution fusion | flops 25787629568 | bytes 106954752 | tf_op jit(solution)/shard_map/dot_general | solution.py:33
  (43 shorter events, 9.0 us)
Async XLA Ops:
  7.2 155.6 %all-gather.5.cloned.1.call-start = ((), (), s32[]{:S(2)}) async-start(), calls=%async_computation.2 | async-start | bytes 10485760 | tf_op jit(solution)/shard_map/all_gather | solution.py:13
  10.3 216.4 %all-reduce.6.cloned.1.call-start = ((), (), s32[]{:S(2)}) async-start(), calls=%async_computation | async-start | bytes 524288 | tf_op jit(solution)/shard_map/psum | solution.py:53
  174.4 214.8 %all-gather.7.cloned.1.call-start = ((), (), s32[]{:S(2)}) async-start(), calls=%async_computation.3 | async-start | bytes 37748736 | tf_op jit(solution)/shard_map/all_gather | solution.py:13
  179.1 354.8 %all-reduce.8.cloned.1.call-start = ((), (), s32[]{:S(2)}) async-start(), calls=%async_computation.1 | async-start | bytes 4194304 | tf_op jit(solution)/shard_map/psum | solution.py:61
  412.0 1.3 copy-start.2
  447.6 196.9 %all-reduce.10.cloned.1.call-start = ((), (), s32[]{:S(2)}) async-start(), calls=%async_computation.4 | async-start | bytes 13107200 | tf_op jit(solution)/shard_map/psum | solution.py:63
  447.7 19.3 %copy-start = (f32[2048,128]{0,1:T(8,128)S(1)}, f32[2048,128]{0,1:T(8,128)}, u32[]{:S(2)}) copy-start(f32[2048,128]{0,1:T(8,128)} %fusion.14) | copy-start | bytes 3145732
  644.5 7.3 copy-start.1
  651.8 31.0 %copy-start.4 = (f32[256,2048]{1,0:T(8,128)S(1)}, f32[256,2048]{1,0:T(8,128)}, u32[]{:S(2)}) copy-start(f32[256,2048]{1,0:T(8,128)} %get-tuple-element.20) | copy-start | bytes 6291460
  682.8 19.2 %copy-start.3 = (f32[2048,256]{0,1:T(8,128)S(1)}, f32[2048,256]{0,1:T(8,128)}, u32[]{:S(2)}) copy-start(f32[2048,256]{0,1:T(8,128)} %all-reduce.8.cloned.1.call-done) | copy-start | bytes 6291460
  682.8 19.2 %copy-start.5 = (f32[256,256]{1,0:T(8,128)S(1)}, f32[256,256]{1,0:T(8,128)}, u32[]{:S(2)}) copy-start(f32[256,256]{1,0:T(8,128)} %get-tuple-element.18) | copy-start | bytes 786436
Sparse Core Ops, SparseCore 0:
  10.4 152.3 all-gather.4
  174.5 52.0 all-reduce.5
  229.1 160.0 all-gather.6
  447.8 86.1 all-reduce.7
  538.6 105.9 all-reduce.9
